TPU v7x, 32 devices: a whole 2x2x4 slice. The times are simulated.
32 devices in a mesh: ctx: 8 (over z, x), wsh: 4 (over y, core).
Axes of the slice: x: 2, y: 2, z: 4, core: 2. Of those that a mesh axis runs over, the one named last changes fastest.
Arguments:
- decoder_in: bfloat16 [4, 1536, 512], P('wsh', 'ctx'), may hold values from -6 to 6
- memory: bfloat16 [4, 2048, 512], P('wsh', 'ctx'), may hold values from -6 to 6
- seq_lengths: int32 [4], P('wsh'), may hold values from 384 to 1536, as said below
- mem_lengths: int32 [4], P('wsh'), may hold values from 1024 to 2048, as said below
- self_query: bfloat16 [512, 512], P('wsh'), may hold values from -0.5 to 0.5
- self_keyval: bfloat16 [512, 1024], P('wsh'), may hold values from -0.25 to 0.25
- self_out: bfloat16 [512, 512], P('wsh'), may hold values from -1.25 to 1.25
- cross_query: bfloat16 [512, 512], P('wsh'), may hold values from -0.5 to 0.5
- cross_keyval: bfloat16 [512, 1024], P('wsh'), may hold values from -0.25 to 0.25
- cross_out: bfloat16 [512, 512], P('wsh'), may hold values from -1.5 to 1.5
- ffn_in: bfloat16 [512, 2048], P('wsh'), may hold values from -0.25 to 0.25
- ffn_bias_in: bfloat16 [2048], P('wsh'), may hold values from -3 to 3
- ffn_out: bfloat16 [2048, 512], P('wsh'), may hold values from -0.125 to 0.125
- ffn_bias_out: bfloat16 [512], P('wsh'), may hold values from -3 to 3
- slot_weight: bfloat16 [1024, 512], P('wsh'), may hold values from -0.1875 to 0.1875
- norm_gain: bfloat16 [3, 512], P(None, 'wsh'), may hold values from 0.099609375 to 1.8984375
- norm_bias: bfloat16 [3, 512], P(None, 'wsh'), may hold values from -3 to 3
- cotangent: bfloat16 [4, 1536, 512], P('wsh', 'ctx'), may hold values from -6 to 6
Outputs:
- slots: bfloat16 [4, 1536, 512], P('wsh', 'ctx')
- grad_input: float32 [4, 1536, 512], P('wsh', 'ctx')
- grad_memory: float32 [4, 2048, 512], P('wsh', 'ctx')
- grad_self_query: float32 [512, 512], P('wsh')
- grad_self_keyval: float32 [512, 1024], P('wsh')
- grad_self_out: float32 [512, 512], P('wsh')
- grad_cross_query: float32 [512, 512], P('wsh')
- grad_cross_keyval: float32 [512, 1024], P('wsh')
- grad_cross_out: float32 [512, 512], P('wsh')
- grad_ffn_in: float32 [512, 2048], P('wsh')
- grad_ffn_bias_in: float32 [2048], P('wsh')
- grad_ffn_out: float32 [2048, 512], P('wsh')
- grad_ffn_bias_out: float32 [512], P('wsh')
- grad_slot_weight: float32 [1024, 512], P('wsh')
- grad_norm_gain: float32 [3, 512], P(None, 'wsh')
- grad_norm_bias: float32 [3, 512], P(None, 'wsh')
Inputs may be any that keep to these rules, and one draw needn't show every extreme that they name: `seq_lengths`: some sequence has all 1536 positions live. `mem_lengths`: some sequence has all 2048 memory rows live.
All inputs are finite; a program needn't handle non-finite values.
Results may differ from a plain program's by a relative error of at most 0.034.
The roundings to bfloat16 on the way count: a program that leaves them out, or rounds other values in their place, can miss the bound.
Values may be sent and summed in bfloat16 or wider, within the bound.
No kernel may reach another device: no remote copies, remote signals or barrier semaphores. Data moves between devices by JAX's collectives and lax.ppermute only.
A program may use at most 256 MiB of HBM per device.

v0:
```python
import math
import jax
import jax.numpy as jnp
from jax import lax
from jax.sharding import PartitionSpec as P

HEADS = 8
NORM_EPS = 1e-05
MASK_FILL = -1e30
HIGH = lax.Precision.HIGHEST


def passed_along(shard, axis, by):
    devices = lax.axis_size(axis)
    pairs = [(i, i + by) for i in range(devices) if 0 <= i + by < devices]
    return lax.ppermute(shard, axis, pairs)


def block_rows(n_rows):
    return math.gcd(n_rows, 1024)


def forward_product(left, weight):
    return jnp.dot(left, weight, preferred_element_type=jnp.float32)


def outer_sum(left, right):
    return lax.dot_general(
        left, right, (((0,), (0,)), ((), ())), preferred_element_type=jnp.float32
    )


def back_product(left, weight):
    return lax.dot_general(
        left, weight, (((1,), (1,)), ((), ())), preferred_element_type=jnp.float32
    )


def norm_forward(values, gain_row, bias_row):
    center = values - jnp.mean(values, axis=-1, keepdims=True)
    inverse = lax.rsqrt(jnp.mean(center * center, axis=-1, keepdims=True) + NORM_EPS)
    normed = center * inverse
    return (normed * gain_row + bias_row, normed, inverse)


def norm_backward(grad_out, normed, inverse, gain_row):
    scaled = grad_out * gain_row
    grad_in = inverse * (
        scaled
        - jnp.mean(scaled, axis=-1, keepdims=True)
        - normed * jnp.mean(scaled * normed, axis=-1, keepdims=True)
    )
    return (grad_in, jnp.sum(grad_out * normed, axis=0), jnp.sum(grad_out, axis=0))


def fold_start(n_rows, n_width):
    head_dim = n_width // HEADS
    return (
        jnp.full((HEADS, n_rows), MASK_FILL, jnp.float32),
        jnp.zeros((HEADS, n_rows), jnp.float32),
        jnp.zeros((n_rows, HEADS, head_dim), jnp.float32),
    )


def fold_keys(state, queries, keyvals, first_key, limit):
    n_rows, n_width = queries.shape
    head_dim = n_width // HEADS
    scaling = head_dim ** (-0.5)
    n_keys = keyvals.shape[0]
    stride = block_rows(n_keys)
    query_heads = queries.reshape(n_rows, HEADS, head_dim)
    blocks = keyvals.reshape(n_keys // stride, stride, 2 * n_width)

    def fold_one_block(carry, item):
        running_max, running_sum, weighted = carry
        block, number = item
        key_part = block[:, :n_width].reshape(stride, HEADS, head_dim)
        value_part = block[:, n_width:].reshape(stride, HEADS, head_dim).astype(jnp.float32)
        scores = (
            jnp.einsum("qhd,khd->hqk", query_heads, key_part, preferred_element_type=jnp.float32)
            * scaling
        )
        places = first_key + number * stride + lax.iota(jnp.int32, stride)
        usable = (places < limit)[None, None, :]
        new_max = jnp.maximum(running_max, jnp.max(jnp.where(usable, scores, MASK_FILL), axis=-1))
        powers = jnp.where(usable, jnp.exp(scores - new_max[:, :, None]), 0.0)
        factor = jnp.exp(running_max - new_max)
        running_sum = running_sum * factor + jnp.sum(powers, axis=-1)
        weighted = weighted * factor.T[:, :, None] + jnp.einsum(
            "hqk,khd->qhd", powers, value_part, precision=HIGH, preferred_element_type=jnp.float32
        )
        return ((new_max, running_sum, weighted), None)

    numbers = jnp.arange(n_keys // stride, dtype=jnp.int32)
    state, unused = lax.scan(fold_one_block, state, (blocks, numbers))
    return state


def fold_finish(state):
    running_max, running_sum, weighted = state
    n_rows = weighted.shape[0]
    mixed = (weighted / running_sum.T[:, :, None]).reshape(n_rows, -1)
    return (mixed, running_max + jnp.log(running_sum))


def row_delta(grad_low, mixed):
    n_rows = mixed.shape[0]
    return jnp.sum((grad_low.astype(jnp.float32) * mixed).reshape(n_rows, HEADS, -1), axis=-1).T


def attend_back(queries, grad_out, log_sums, deltas, keyvals, limit):
    n_rows, n_width = queries.shape
    head_dim = n_width // HEADS
    scaling = head_dim ** (-0.5)
    n_keys = keyvals.shape[0]
    stride = block_rows(n_keys)
    query_heads = queries.reshape(n_rows, HEADS, head_dim)
    grad_heads = grad_out.reshape(n_rows, HEADS, head_dim)
    grad_wide = grad_heads.astype(jnp.float32)
    blocks = keyvals.reshape(n_keys // stride, stride, 2 * n_width)

    def attend_one_block(carry, item):
        block, number = item
        key_part = block[:, :n_width].reshape(stride, HEADS, head_dim)
        value_part = block[:, n_width:].reshape(stride, HEADS, head_dim)
        scores = (
            jnp.einsum("qhd,khd->hqk", query_heads, key_part, preferred_element_type=jnp.float32)
            * scaling
        )
        places = number * stride + lax.iota(jnp.int32, stride)
        usable = (places < limit)[None, None, :]
        probs = jnp.where(usable, jnp.exp(scores - log_sums[:, :, None]), 0.0)
        d_probs = jnp.einsum(
            "qhd,khd->hqk", grad_heads, value_part, preferred_element_type=jnp.float32
        )
        d_scores = (probs * (d_probs - deltas[:, :, None])).astype(jnp.bfloat16)
        carry = (
            carry
            + jnp.einsum("hqk,khd->qhd", d_scores, key_part, preferred_element_type=jnp.float32)
            * scaling
        )
        d_keys = (
            jnp.einsum("hqk,qhd->khd", d_scores, query_heads, preferred_element_type=jnp.float32)
            * scaling
        )
        d_values = jnp.einsum(
            "hqk,qhd->khd", probs, grad_wide, precision=HIGH, preferred_element_type=jnp.float32
        )
        return (
            carry,
            jnp.concatenate(
                [d_keys.reshape(stride, n_width), d_values.reshape(stride, n_width)], axis=1
            ),
        )

    numbers = jnp.arange(n_keys // stride, dtype=jnp.int32)
    start_grad = jnp.zeros((n_rows, HEADS, head_dim), jnp.float32)
    d_query, key_terms = lax.scan(attend_one_block, start_grad, (blocks, numbers))
    return (d_query.reshape(n_rows, n_width), key_terms.reshape(n_keys, 2 * n_width))


def shards(
    decoder_in,
    memory,
    seq_lengths,
    mem_lengths,
    self_query,
    self_keyval,
    self_out,
    cross_query,
    cross_keyval,
    cross_out,
    ffn_in,
    ffn_bias_in,
    ffn_out,
    ffn_bias_out,
    slot_weight,
    norm_gain,
    norm_bias,
    cotangent,
):
    gathered = (
        lax.all_gather(self_query, "wsh", axis=0, tiled=True),
        lax.all_gather(self_keyval, "wsh", axis=0, tiled=True),
        lax.all_gather(self_out, "wsh", axis=0, tiled=True),
        lax.all_gather(cross_query, "wsh", axis=0, tiled=True),
        lax.all_gather(cross_keyval, "wsh", axis=0, tiled=True),
        lax.all_gather(cross_out, "wsh", axis=0, tiled=True),
        lax.all_gather(ffn_in, "wsh", axis=0, tiled=True),
        lax.all_gather(ffn_bias_in, "wsh", axis=0, tiled=True),
        lax.all_gather(ffn_out, "wsh", axis=0, tiled=True),
        lax.all_gather(ffn_bias_out, "wsh", axis=0, tiled=True),
        lax.all_gather(slot_weight, "wsh", axis=0, tiled=True),
        lax.all_gather(norm_gain, "wsh", axis=1, tiled=True),
        lax.all_gather(norm_bias, "wsh", axis=1, tiled=True),
    )
    (
        w_query,
        w_keyval,
        w_out,
        c_query,
        c_keyval,
        c_out,
        w_first,
        b_first,
        w_second,
        b_second,
        w_slot,
        gains,
        biases,
    ) = gathered
    tokens = decoder_in[0]
    n_rows, n_width = tokens.shape
    live_count = seq_lengths[0]
    mem_count = mem_lengths[0]
    places = lax.axis_index("ctx") * n_rows + lax.iota(jnp.int32, n_rows)
    live = (places < live_count)[:, None]
    valid = live.astype(jnp.float32)
    gains = gains.astype(jnp.float32)
    biases = biases.astype(jnp.float32)
    queries = forward_product(tokens, w_query).astype(jnp.bfloat16)
    keyvals = forward_product(tokens, w_keyval).astype(jnp.bfloat16)
    self_state = fold_keys(
        fold_start(n_rows, n_width),
        queries,
        lax.all_gather(keyvals, "ctx", axis=0, tiled=True),
        jnp.int32(0),
        live_count,
    )
    self_mixed, self_lse = fold_finish(self_state)
    self_low = self_mixed.astype(jnp.bfloat16)
    first_sum = tokens.astype(jnp.float32) + forward_product(self_low, w_out)
    hidden_one, normed_one, inverse_one = norm_forward(first_sum, gains[0], biases[0])
    hidden_one_low = hidden_one.astype(jnp.bfloat16)
    cross_queries = forward_product(hidden_one_low, c_query).astype(jnp.bfloat16)
    mem_rows = memory[0]
    mem_keyvals = forward_product(mem_rows, c_keyval).astype(jnp.bfloat16)
    mem_all = lax.all_gather(mem_keyvals, "ctx", axis=0, tiled=True)
    cross_state = fold_keys(fold_start(n_rows, n_width), cross_queries, mem_all, 0, mem_count)
    cross_mixed, cross_lse = fold_finish(cross_state)
    cross_low = cross_mixed.astype(jnp.bfloat16)
    second_sum = hidden_one + forward_product(cross_low, c_out)
    hidden_two, normed_two, inverse_two = norm_forward(second_sum, gains[1], biases[1])
    hidden_two_low = hidden_two.astype(jnp.bfloat16)
    preact = forward_product(hidden_two_low, w_first) + b_first.astype(jnp.float32)
    active_wide, gelu_pull = jax.vjp(jax.nn.gelu, preact)
    active = active_wide.astype(jnp.bfloat16)
    third_sum = hidden_two + forward_product(active, w_second) + b_second.astype(jnp.float32)
    hidden_three, normed_three, inverse_three = norm_forward(third_sum, gains[2], biases[2])
    masked_low = (hidden_three * valid).astype(jnp.bfloat16)
    next_row = passed_along(masked_low[:1], "ctx", -1)
    paired = jnp.concatenate(
        [masked_low, jnp.concatenate([masked_low[1:], next_row], axis=0)], axis=1
    )
    slots = (forward_product(paired, w_slot) * valid).astype(jnp.bfloat16)
    grad_slots = jnp.where(live, cotangent[0], jnp.zeros_like(cotangent[0]))
    g_slot = outer_sum(paired, grad_slots)
    d_paired = back_product(grad_slots, w_slot)
    d_own = d_paired[:, :n_width]
    d_next = d_paired[:, n_width:]
    carried = passed_along(d_next[-1:], "ctx", 1)
    d_three = (d_own + jnp.concatenate([carried, d_next[:-1]], axis=0)) * valid
    d_third, g_gain_three, g_bias_three = norm_backward(
        d_three, normed_three, inverse_three, gains[2]
    )
    e_third = d_third.astype(jnp.bfloat16)
    g_second = outer_sum(active, e_third)
    g_bsecond = jnp.sum(e_third.astype(jnp.float32), axis=0)
    d_pre = gelu_pull(back_product(e_third, w_second))[0].astype(jnp.bfloat16)
    g_bfirst = jnp.sum(d_pre.astype(jnp.float32), axis=0)
    g_first = outer_sum(hidden_two_low, d_pre)
    d_two = d_third + back_product(d_pre, w_first)
    d_second, g_gain_two, g_bias_two = norm_backward(d_two, normed_two, inverse_two, gains[1])
    e_second = d_second.astype(jnp.bfloat16)
    g_cout = outer_sum(cross_low, e_second)
    d_cross = back_product(e_second, c_out).astype(jnp.bfloat16)
    d_cq, mem_terms = attend_back(
        cross_queries, d_cross, cross_lse, row_delta(d_cross, cross_mixed), mem_all, mem_count
    )
    d_memkv = lax.psum_scatter(mem_terms, "ctx", scatter_dimension=0, tiled=True).astype(
        jnp.bfloat16
    )
    g_ckv = outer_sum(mem_rows, d_memkv)
    grad_memory = back_product(d_memkv, c_keyval)
    d_cq_low = d_cq.astype(jnp.bfloat16)
    g_cquery = outer_sum(hidden_one_low, d_cq_low)
    d_one = d_second + back_product(d_cq_low, c_query)
    d_first, g_gain_one, g_bias_one = norm_backward(d_one, normed_one, inverse_one, gains[0])
    e_first = d_first.astype(jnp.bfloat16)
    g_out = outer_sum(self_low, e_first)
    d_self = back_product(e_first, w_out).astype(jnp.bfloat16)
    keyval_back = lax.all_gather(keyvals, "ctx", axis=0, tiled=True)
    self_delta = row_delta(d_self, self_mixed)
    d_query, key_terms = attend_back(queries, d_self, self_lse, self_delta, keyval_back, live_count)
    d_kv = lax.psum_scatter(key_terms, "ctx", scatter_dimension=0, tiled=True).astype(jnp.bfloat16)
    d_query_low = d_query.astype(jnp.bfloat16)
    g_query = outer_sum(tokens, d_query_low)
    g_keyval = outer_sum(tokens, d_kv)
    grad_input = d_first + back_product(d_query_low, w_query) + back_product(d_kv, w_keyval)
    g_gains = jnp.stack([g_gain_one, g_gain_two, g_gain_three])
    g_biases = jnp.stack([g_bias_one, g_bias_two, g_bias_three])
    summed = lax.psum(
        (
            g_query,
            g_keyval,
            g_out,
            g_cquery,
            g_ckv,
            g_cout,
            g_first,
            g_bfirst,
            g_second,
            g_bsecond,
            g_slot,
            g_gains,
            g_biases,
        ),
        "ctx",
    )
    shares = (
        lax.psum_scatter(
            summed[0].astype(jnp.bfloat16), "wsh", scatter_dimension=0, tiled=True
        ).astype(jnp.float32),
        lax.psum_scatter(
            summed[1].astype(jnp.bfloat16), "wsh", scatter_dimension=0, tiled=True
        ).astype(jnp.float32),
        lax.psum_scatter(
            summed[2].astype(jnp.bfloat16), "wsh", scatter_dimension=0, tiled=True
        ).astype(jnp.float32),
        lax.psum_scatter(
            summed[3].astype(jnp.bfloat16), "wsh", scatter_dimension=0, tiled=True
        ).astype(jnp.float32),
        lax.psum_scatter(
            summed[4].astype(jnp.bfloat16), "wsh", scatter_dimension=0, tiled=True
        ).astype(jnp.float32),
        lax.psum_scatter(
            summed[5].astype(jnp.bfloat16), "wsh", scatter_dimension=0, tiled=True
        ).astype(jnp.float32),
        lax.psum_scatter(
            summed[6].astype(jnp.bfloat16), "wsh", scatter_dimension=0, tiled=True
        ).astype(jnp.float32),
        lax.psum_scatter(
            summed[7].astype(jnp.bfloat16), "wsh", scatter_dimension=0, tiled=True
        ).astype(jnp.float32),
        lax.psum_scatter(
            summed[8].astype(jnp.bfloat16), "wsh", scatter_dimension=0, tiled=True
        ).astype(jnp.float32),
        lax.psum_scatter(
            summed[9].astype(jnp.bfloat16), "wsh", scatter_dimension=0, tiled=True
        ).astype(jnp.float32),
        lax.psum_scatter(
            summed[10].astype(jnp.bfloat16), "wsh", scatter_dimension=0, tiled=True
        ).astype(jnp.float32),
        lax.psum_scatter(
            summed[11].astype(jnp.bfloat16), "wsh", scatter_dimension=1, tiled=True
        ).astype(jnp.float32),
        lax.psum_scatter(
            summed[12].astype(jnp.bfloat16), "wsh", scatter_dimension=1, tiled=True
        ).astype(jnp.float32),
    )
    return (
        slots[None],
        grad_input[None],
        grad_memory[None],
        shares[0],
        shares[1],
        shares[2],
        shares[3],
        shares[4],
        shares[5],
        shares[6],
        shares[7],
        shares[8],
        shares[9],
        shares[10],
        shares[11],
        shares[12],
    )


def solution(mesh):
    in_specs = (
        P("wsh", "ctx", None),
        P("wsh", "ctx", None),
        P("wsh"),
        P("wsh"),
        P("wsh", None),
        P("wsh", None),
        P("wsh", None),
        P("wsh", None),
        P("wsh", None),
        P("wsh", None),
        P("wsh", None),
        P("wsh"),
        P("wsh", None),
        P("wsh"),
        P("wsh", None),
        P(None, "wsh"),
        P(None, "wsh"),
        P("wsh", "ctx", None),
    )
    out_specs = (
        P("wsh", "ctx", None),
        P("wsh", "ctx", None),
        P("wsh", "ctx", None),
        P("wsh", None),
        P("wsh", None),
        P("wsh", None),
        P("wsh", None),
        P("wsh", None),
        P("wsh", None),
        P("wsh", None),
        P("wsh"),
        P("wsh", None),
        P("wsh"),
        P("wsh", None),
        P(None, "wsh"),
        P(None, "wsh"),
    )
    return jax.shard_map(shards, mesh=mesh, in_specs=in_specs, out_specs=out_specs, check_vma=False)
```

profile of v0, /device:TPU:0, one launch (start us, length us, event | category | flops | bytes accessed | tf_op | source)
XLA Modules:
  0.0 1701.6 jit_solution(16746929962556680504)
XLA Ops:
  9.5 19.6 %all-gather.10.cloned.1.call-done = bf16[512,1024]{1,0:T(8,128)(2,1)} async-done(((bf16[128,1024]{1,0:T(8,128)(2,1)}), bf16[512,1024]{1,0:T(8,128)(2,1)}) %all-gather.10.cloned.1.call-update) | async-done | bytes 1048592 | tf_op jit(solution)/shard_map/all_gather | solution.py:184
  31.6 15.8 all-gather.14.cloned.1.call-done
  52.0 5.0 all-gather.1
  57.7 5.2 all-gather
  63.4 7.7 all_gather.55
  71.1 7.7 all_gather.54
  78.8 7.7 all_gather.49
  86.6 7.3 all_gather.48
  95.8 5.1 all_gather.51
  101.4 5.1 all_gather.50
  110.9 4.4 collective-permute-start.1
  115.4 13.5 all-gather.12.cloned.1.call-done
  128.9 4.7 copy.69
  133.5 27.7 %while.56 = (s32[]{:T(128)}, f32[8,192]{1,0:T(8,128)S(1)}, f32[8,192]{1,0:T(8,128)S(1)}, f32[192,8,64]{0,2,1:T(8,128)}, s32[3]{0:T(128)S(1)}, /*index=5*/s32[]{:...) while((s32[]{:T(128)}, f32[8,192]{1,0:T(8,128)S(1)}, ...), condition=%wide.region_3.4_spmd.clone, body=%wide.region_0.3_spmd.clone.sunk | while | flops 712812544 | bytes 21793044 | solution.py:95
  166.4 37.1 %all-gather.16.cloned.1.call-done = bf16[2048,1024]{1,0:T(8,128)(2,1)} async-done(((bf16[256,1024]{1,0:T(8,128)(2,1)}), bf16[2048,1024]{1,0:T(8,128)(2,1)}) %all-gather.16.cloned.1.call-update) | async-done | bytes 4194320 | tf_op jit(solution)/shard_map/all_gather | solution.py:238
  203.5 6.3 copy.71
  209.8 34.2 %while.57 = (s32[]{:T(128)}, f32[8,192]{1,0:T(8,128)S(1)}, f32[8,192]{1,0:T(8,128)S(1)}, f32[192,8,64]{0,2,1:T(8,128)S(1)}, s32[2]{0:T(128)S(1)}, /*index=5*/s32...) while((s32[]{:T(128)}, f32[8,192]{1,0:T(8,128)S(1)}, ...), condition=%wide.region_9.10_spmd.clone, body=%wide.region_6.9_spmd.clone.sunk | while | flops 1425320960 | bytes 55611584 | solution.py:95
  213.7 3.7 select_reduce_fusion.5
  217.4 4.0 fusion.210
  222.1 4.6 fusion.212
  230.6 3.7 select_reduce_fusion.5
  234.3 4.1 fusion.210
  239.3 4.6 fusion.212
  254.9 2.8 multiply_reduce_fusion
  259.5 3.9 convert_reduce_fusion
  268.1 67.6 %while.58 = (s32[]{:T(128)}, f32[192,8,64]{0,2,1:T(8,128)}, f32[2,1024,1024]{2,1,0:T(8,128)}, bf16[2,1024,1024]{1,2,0:T(8,128)(2,1)}, s32[2]{0:T(128)S(1)}, /*in...) while((s32[]{:T(128)}, f32[192,8,64]{0,2,1:T(8,128)}, ...), condition=%wide.region_20.21_spmd.clone, body=%wide.region_19.20_spmd.clone.sunk | while | flops 2029291520 | bytes 105100704 | solution.py:158
  273.4 3.3 multiply_convert_fusion.8
  276.7 3.2 fusion.224
  279.9 7.5 fusion.225
  291.6 5.4 copy.123
  297.0 4.8 constant_dynamic-update-slice_fusion.4
  307.1 3.3 multiply_convert_fusion.8
  310.4 3.3 fusion.224
  313.7 7.4 fusion.225
  325.4 5.4 copy.123
  330.8 4.8 constant_dynamic-update-slice_fusion.4
  344.5 57.7 %while.59 = (s32[]{:T(128)}, f32[192,8,64]{0,2,1:T(8,128)}, f32[3,512,1024]{2,1,0:T(8,128)}, bf16[3,512,1024]{1,2,0:T(8,128)(2,1)}, s32[3]{0:T(128)S(1)}, /*inde...) while((s32[]{:T(128)}, f32[192,8,64]{0,2,1:T(8,128)}, ...), condition=%wide.region_25.26_spmd.clone, body=%wide.region_24.25_spmd.clone.sunk | while | flops 1014793216 | bytes 47927116 | solution.py:158
  349.6 3.1 multiply_convert_fusion.9
  352.7 3.0 fusion.237
  355.8 2.7 fusion.238
  368.6 3.1 multiply_convert_fusion.9
  371.8 3.1 fusion.237
  374.9 2.7 fusion.238
  387.9 3.1 multiply_convert_fusion.9
  391.1 3.1 fusion.237
  394.2 2.7 fusion.238
  411.8 2.8 fusion.88
  414.7 2.8 fusion.80
  418.7 101.6 %reduce-scatter.24.cloned.1.call-done = f32[192,1024]{1,0:T(8,128)} async-done(((f32[1536,1024]{1,0:T(8,128)}), f32[192,1024]{1,0:T(8,128)}) %reduce-scatter.24.cloned.1.call-update) | async-done | bytes 786448 | tf_op jit(solution)/shard_map/reduce_scatter | solution.py:295
  520.4 2.9 convolution_bitcast_fusion.1
  523.3 148.9 %reduce-scatter.26.cloned.1.call-done = f32[256,1024]{1,0:T(8,128)} async-done(((f32[2048,1024]{1,0:T(8,128)}), f32[256,1024]{1,0:T(8,128)}) %reduce-scatter.26.cloned.1.call-update) | async-done | bytes 1048592 | tf_op jit(solution)/shard_map/reduce_scatter | solution.py:280
  672.2 3.1 convolution_bitcast_fusion
  675.3 726.0 %all-reduce.5 = (bf16[512,512]{0,1:T(8,128)(2,1)}, bf16[512,1024]{0,1:T(8,128)(2,1)}, bf16[512,1024]{0,1:T(8,128)(2,1)}, bf16[512,512]{1,0:T(8,128)(2,1)}, bf16[...) all-reduce(f32[512,512]{0,1:T(8,128)} %convolution_bitcast_fusion.2, ...), channel_id=1, replica_groups=mesh['ctx'=8,'wsh'=4] {'ctx'}, use_global_device_ids=true, to_apply=%region_28.29 | all-reduce | flops 4724224 | bytes 28345344 | tf_op jit(solution)/shard_map/psum | solution.py:302
  1419.6 6.9 all-reduce.3
  1430.5 12.7 reduce-scatter.48.cloned.1.call-done
  1444.6 22.8 %reduce-scatter.40.cloned.1.call-done = bf16[128,512]{1,0:T(8,128)(2,1)} async-done(((bf16[512,512]{1,0:T(8,128)(2,1)}), bf16[128,512]{1,0:T(8,128)(2,1)}) %reduce-scatter.40.cloned.1.call-update) | async-done | bytes 131088
  1469.3 22.9 %reduce-scatter.28.cloned.1.call-done = bf16[128,512]{1,0:T(8,128)(2,1)} async-done(((bf16[512,512]{1,0:T(8,128)(2,1)}), bf16[128,512]{1,0:T(8,128)(2,1)}) %reduce-scatter.28.cloned.1.call-update) | async-done | bytes 131088 | tf_op jit(solution)/shard_map/reduce_scatter | solution.py:327
  1493.8 23.2 %reduce-scatter.30.cloned.1.call-done = bf16[128,512]{1,0:T(8,128)(2,1)} async-done(((bf16[512,512]{1,0:T(8,128)(2,1)}), bf16[128,512]{1,0:T(8,128)(2,1)}) %reduce-scatter.30.cloned.1.call-update) | async-done | bytes 131088 | tf_op jit(solution)/shard_map/reduce_scatter | solution.py:330
  1518.6 22.4 %reduce-scatter.32.cloned.1.call-done = bf16[128,512]{1,0:T(8,128)(2,1)} async-done(((bf16[512,512]{1,0:T(8,128)(2,1)}), bf16[128,512]{1,0:T(8,128)(2,1)}) %reduce-scatter.32.cloned.1.call-update) | async-done | bytes 131088 | tf_op jit(solution)/shard_map/reduce_scatter | solution.py:336
  1542.6 26.4 %reduce-scatter.42.cloned.1.call-done = bf16[128,1024]{1,0:T(8,128)(2,1)} async-done(((bf16[512,1024]{1,0:T(8,128)(2,1)}), bf16[128,1024]{1,0:T(8,128)(2,1)}) %reduce-scatter.42.cloned.1.call-update) | async-done | bytes 262160
  1571.1 25.8 %reduce-scatter.44.cloned.1.call-done = bf16[128,1024]{1,0:T(8,128)(2,1)} async-done(((bf16[512,1024]{1,0:T(8,128)(2,1)}), bf16[128,1024]{1,0:T(8,128)(2,1)}) %reduce-scatter.44.cloned.1.call-update) | async-done | bytes 262160
  1599.0 25.4 %reduce-scatter.38.cloned.1.call-done = bf16[256,512]{1,0:T(8,128)(2,1)} async-done(((bf16[1024,512]{1,0:T(8,128)(2,1)}), bf16[256,512]{1,0:T(8,128)(2,1)}) %reduce-scatter.38.cloned.1.call-update) | async-done | bytes 262160 | tf_op jit(solution)/shard_map/reduce_scatter | solution.py:351
  1626.2 32.1 %reduce-scatter.34.cloned.1.call-done = bf16[128,2048]{1,0:T(8,128)(2,1)} async-done(((bf16[512,2048]{1,0:T(8,128)(2,1)}), bf16[128,2048]{1,0:T(8,128)(2,1)}) %reduce-scatter.34.cloned.1.call-update) | async-done | bytes 524304 | tf_op jit(solution)/shard_map/reduce_scatter | solution.py:339
  1660.4 31.9 %reduce-scatter.36.cloned.1.call-done = bf16[512,512]{1,0:T(8,128)(2,1)} async-done(((bf16[2048,512]{1,0:T(8,128)(2,1)}), bf16[512,512]{1,0:T(8,128)(2,1)}) %reduce-scatter.36.cloned.1.call-update) | async-done | bytes 524304 | tf_op jit(solution)/shard_map/reduce_scatter | solution.py:345
  (501 shorter events, 176.7 us)
Async XLA Ops:
  7.2 40.2 %copy-start = (bf16[1,256,512]{2,1,0:T(8,128)(2,1)S(1)}, bf16[1,256,512]{2,1,0:T(8,128)(2,1)}, u32[]{:S(2)}) copy-start(bf16[1,256,512]{2,1,0:T(8,128)(2,1)} %param.27) | copy-start | bytes 786436
  7.2 44.8 %copy-start.102 = (bf16[128]{0:T(256)(128)(2,1)S(1)}, bf16[128]{0:T(256)(128)(2,1)}, u32[]{:S(2)}) copy-start(bf16[128]{0:T(256)(128)(2,1)} %param.39) | copy-start | bytes 772
  7.2 50.4 %copy-start.99 = (bf16[512]{0:T(512)(128)(2,1)S(1)}, bf16[512]{0:T(512)(128)(2,1)}, u32[]{:S(2)}) copy-start(bf16[512]{0:T(512)(128)(2,1)} %param.37) | copy-start | bytes 3076
  7.2 56.2 %copy-start.64 = (bf16[128,512]{1,0:T(8,128)(2,1)S(1)}, bf16[128,512]{1,0:T(8,128)(2,1)}, u32[]{:S(2)}) copy-start(bf16[128,512]{1,0:T(8,128)(2,1)} %param.35) | copy-start | bytes 393220
  7.2 21.9 %all-gather.10.cloned.1.call-start = ((), (), s32[]{:S(2)}) async-start(), calls=%async_computation.13 | async-start | bytes 1310720 | tf_op jit(solution)/shard_map/all_gather | solution.py:184
  8.0 39.4 %all-gather.14.cloned.1.call-start = ((), (), s32[]{:S(2)}) async-start(), calls=%async_computation.15 | async-start | bytes 1310720 | tf_op jit(solution)/shard_map/all_gather | solution.py:187
  8.7 98.9 %all-gather.22.cloned.1.call-start = ((), (), s32[]{:S(2)}) async-start(), calls=%async_computation.19 | async-start | bytes 1310720 | tf_op jit(solution)/shard_map/all_gather | solution.py:193
  9.4 61.7 %copy-start.65 = (bf16[128,512]{1,0:T(8,128)(2,1)S(1)}, bf16[128,512]{1,0:T(8,128)(2,1)}, u32[]{:S(2)}) copy-start(bf16[128,512]{1,0:T(8,128)(2,1)} %param.33) | copy-start | bytes 393220
  9.5 69.4 %copy-start.66 = (bf16[128,512]{1,0:T(8,128)(2,1)S(1)}, bf16[128,512]{1,0:T(8,128)(2,1)}, u32[]{:S(2)}) copy-start(bf16[128,512]{1,0:T(8,128)(2,1)} %param.32) | copy-start | bytes 393220
  9.5 119.4 %all-gather.12.cloned.1.call-start = ((), (), s32[]{:S(2)}) async-start(), calls=%async_computation.14 | async-start | bytes 3538944 | tf_op jit(solution)/shard_map/all_gather | solution.py:226
  31.5 55.0 %copy-start.67 = (bf16[128,512]{1,0:T(8,128)(2,1)S(1)}, bf16[128,512]{1,0:T(8,128)(2,1)}, u32[]{:S(2)}) copy-start(bf16[128,512]{1,0:T(8,128)(2,1)} %param.30) | copy-start | bytes 393220
  31.6 63.1 %copy-start.29 = (bf16[1,192,512]{2,1,0:T(8,128)(2,1)S(1)}, bf16[1,192,512]{2,1,0:T(8,128)(2,1)}, u32[]{:S(2)}) copy-start(bf16[1,192,512]{2,1,0:T(8,128)(2,1)} %param.26) | copy-start | bytes 589828
  31.6 171.9 %all-gather.16.cloned.1.call-start = ((), (), s32[]{:S(2)}) async-start(), calls=%async_computation.16 | async-start | bytes 4718592 | tf_op jit(solution)/shard_map/all_gather | solution.py:238
  49.9 45.9 %copy-start.100 = (bf16[3,128]{1,0:T(4,128)(2,1)S(1)}, bf16[3,128]{1,0:T(4,128)(2,1)}, u32[]{:S(2)}) copy-start(bf16[3,128]{1,0:T(4,128)(2,1)} %param.42) | copy-start | bytes 2308
  49.9 51.5 %copy-start.101 = (bf16[3,128]{1,0:T(4,128)(2,1)S(1)}, bf16[3,128]{1,0:T(4,128)(2,1)}, u32[]{:S(2)}) copy-start(bf16[3,128]{1,0:T(4,128)(2,1)} %param.41) | copy-start | bytes 2308
  49.9 57.8 %copy-start.54 = (bf16[1,192,512]{2,1,0:T(8,128)(2,1)S(1)}, bf16[1,192,512]{2,1,0:T(8,128)(2,1)}, u32[]{:S(2)}) copy-start(bf16[1,192,512]{2,1,0:T(8,128)(2,1)} %param.43) | copy-start | bytes 589828
  49.9 195.5 %all-gather.18.cloned.1.call-start = ((), (), s32[]{:S(2)}) async-start(), calls=%async_computation.17 | async-start | bytes 2621440 | tf_op jit(solution)/shard_map/all_gather | solution.py:189
  50.5 199.6 %all-gather.20.cloned.1.call-start = ((), (), s32[]{:S(2)}) async-start(), calls=%async_computation.18 | async-start | bytes 2621440 | tf_op jit(solution)/shard_map/all_gather | solution.py:191
  51.2 469.2 %reduce-scatter.24.cloned.1.call-start = ((), (), s32[]{:S(2)}) async-start(), calls=%async_computation.20 | async-start | bytes 7077888 | tf_op jit(solution)/shard_map/reduce_scatter | solution.py:295
  101.4 63.9 %copy-start.82 = (f32[1,512]{1,0:T(1,128)}, f32[1,512]{1,0:T(1,128)S(1)}, u32[]{:S(2)}) copy-start(f32[1,512]{1,0:T(1,128)S(1)} %get-tuple-element.648) | copy-start | bytes 6148
  107.1 58.2 %copy-start.69 = (f32[1,512]{1,0:T(1,128)}, f32[1,512]{1,0:T(1,128)S(1)}, u32[]{:S(2)}) copy-start(f32[1,512]{1,0:T(1,128)S(1)} %get-tuple-element.645) | copy-start | bytes 6148
  107.6 25.9 %copy-start.94 = (pred[192]{0:T(512)(128)(4,1)}, pred[192]{0:T(512)(128)(4,1)S(1)}, u32[]{:S(2)}) copy-start(pred[192]{0:T(512)(128)(4,1)S(1)} %get-tuple-element.629) | copy-start | bytes 580
  110.9 144.0 %collective-permute-start.1 = (f32[1,512]{1,0:T(1,128)}, f32[1,512]{1,0:T(1,128)}, u32[]{:S(2)}, u32[]{:S(2)}) collective-permute-start(f32[1,512]{1,0:T(1,128)} %slice.99), channel_id=1, source_target_pairs={{0,4},{4,8},{8,12},{12,16},{16,20},{20,24},{24,28},{1,5},{5,9},{9,... | collective-permute-start | bytes 6152 | tf_op jit(solution)/shard_map/ppermute | solution.py:16
  165.0 79.1 %copy-start.11 = (f32[192,512]{1,0:T(8,128)}, f32[192,512]{1,0:T(8,128)S(1)}, u32[]{:S(2)}) copy-start(f32[192,512]{1,0:T(8,128)S(1)} %get-tuple-element.650) | copy-start | bytes 1179652
  165.1 79.1 %copy-start.75 = (f32[192]{0:T(256)}, f32[192]{0:T(256)S(1)}, u32[]{:S(2)}) copy-start(f32[192]{0:T(256)S(1)} %broadcast_multiply_fusion.8) | copy-start | bytes 2308
  165.3 78.9 %copy-start.79 = (f32[192]{0:T(256)}, f32[192]{0:T(256)S(1)}, u32[]{:S(2)}) copy-start(f32[192]{0:T(256)S(1)} %add_rsqrt_fusion.2) | copy-start | bytes 2308
  203.5 6.3 copy-start.58
  209.8 34.4 %copy-start.35 = (bf16[512,512]{1,0:T(8,128)(2,1)S(1)}, bf16[512,512]{1,0:T(8,128)(2,1)}, u32[]{:S(2)}) copy-start(bf16[512,512]{1,0:T(8,128)(2,1)} %all_gather.55) | copy-start | bytes 1572868
  209.8 34.4 %copy-start.70 = (f32[1,512]{1,0:T(1,128)S(1)}, f32[1,512]{1,0:T(1,128)}, u32[]{:S(2)}) copy-start(f32[1,512]{1,0:T(1,128)} %copy-done.69) | copy-start | bytes 6148
  209.8 34.4 %copy-start.83 = (f32[1,512]{1,0:T(1,128)S(1)}, f32[1,512]{1,0:T(1,128)}, u32[]{:S(2)}) copy-start(f32[1,512]{1,0:T(1,128)} %copy-done.82) | copy-start | bytes 6148
  244.1 9.8 copy-start.21
  244.6 20.9 %copy-start.15 = (f32[192,512]{1,0:T(8,128)}, f32[192,512]{1,0:T(8,128)S(1)}, u32[]{:S(2)}) copy-start(f32[192,512]{1,0:T(8,128)S(1)} %get-tuple-element.652) | copy-start | bytes 1179652
  247.7 11.8 copy-start.23
  268.1 68.8 %copy-start.71 = (f32[1,512]{1,0:T(1,128)S(1)}, f32[1,512]{1,0:T(1,128)}, u32[]{:S(2)}) copy-start(f32[1,512]{1,0:T(1,128)} %copy-done.69) | copy-start | bytes 6148
  268.1 68.8 %copy-start.76 = (f32[192]{0:T(256)S(1)}, f32[192]{0:T(256)}, u32[]{:S(2)}) copy-start(f32[192]{0:T(256)} %copy-done.75) | copy-start | bytes 2308
  268.1 68.8 %copy-start.80 = (f32[192]{0:T(256)S(1)}, f32[192]{0:T(256)}, u32[]{:S(2)}) copy-start(f32[192]{0:T(256)} %copy-done.79) | copy-start | bytes 2308
  335.6 5.6 copy-start.34
  335.6 5.6 copy-start.48
  402.2 269.9 %reduce-scatter.26.cloned.1.call-start = ((), (), s32[]{:S(2)}) async-start(), calls=%async_computation.21 | async-start | bytes 9437184 | tf_op jit(solution)/shard_map/reduce_scatter | solution.py:280
  403.0 6.3 copy-start.20
  403.0 6.2 copy-start.26
  403.0 7.5 copy-start.22
  403.0 7.5 copy-start.28
  403.0 1026.0 %reduce-scatter.46.cloned.1.call-start = ((), (), s32[]{:S(2)}) async-start(), calls=%async_computation.31 | async-start | bytes 163840
  403.2 14.3 collective-permute-start
  404.7 5.8 copy-start.45
  417.5 257.7 %copy-start.56 = (bf16[191,512]{1,0:T(8,128)(2,1)}, bf16[191,512]{1,0:T(8,128)(2,1)S(1)}, u32[]{:S(2)}) copy-start(bf16[191,512]{1,0:T(8,128)(2,1)S(1)} %slice.96) | copy-start | bytes 586756
  418.7 256.6 %copy-start.81 = (f32[3,512]{1,0:T(4,128)S(1)}, f32[3,512]{1,0:T(4,128)}, u32[]{:S(2)}) copy-start(f32[3,512]{1,0:T(4,128)} %pad_maximum_fusion) | copy-start | bytes 18436
  418.7 256.5 %copy-start.88 = (f32[2048]{0:T(1024)S(1)}, f32[2048]{0:T(1024)}, u32[]{:S(2)}) copy-start(f32[2048]{0:T(1024)} %get-tuple-element.661) | copy-start | bytes 24580
  418.7 256.5 %copy-start.93 = (f32[512]{0:T(512)S(1)}, f32[512]{0:T(512)}, u32[]{:S(2)}) copy-start(f32[512]{0:T(512)} %get-tuple-element.625) | copy-start | bytes 6148
  1401.2 5.9 copy-start.53
  1402.1 41.1 %reduce-scatter.48.cloned.1.call-start = ((), (), s32[]{:S(2)}) async-start(), calls=%async_computation.32 | async-start | bytes 163840
  1402.9 64.5 %reduce-scatter.40.cloned.1.call-start = ((), (), s32[]{:S(2)}) async-start(), calls=%async_computation.28 | async-start | bytes 655360
  1403.0 5.8 copy-start.52
  1405.2 87.0 %reduce-scatter.28.cloned.1.call-start = ((), (), s32[]{:S(2)}) async-start(), calls=%async_computation.22 | async-start | bytes 655360 | tf_op jit(solution)/shard_map/reduce_scatter | solution.py:327
  1405.9 111.0 %reduce-scatter.30.cloned.1.call-start = ((), (), s32[]{:S(2)}) async-start(), calls=%async_computation.23 | async-start | bytes 655360 | tf_op jit(solution)/shard_map/reduce_scatter | solution.py:330
  1406.5 134.5 %reduce-scatter.32.cloned.1.call-start = ((), (), s32[]{:S(2)}) async-start(), calls=%async_computation.24 | async-start | bytes 655360 | tf_op jit(solution)/shard_map/reduce_scatter | solution.py:336
  1407.1 161.9 %reduce-scatter.42.cloned.1.call-start = ((), (), s32[]{:S(2)}) async-start(), calls=%async_computation.29 | async-start | bytes 1310720
  1408.7 188.2 %reduce-scatter.44.cloned.1.call-start = ((), (), s32[]{:S(2)}) async-start(), calls=%async_computation.30 | async-start | bytes 1310720
  1410.2 214.2 %reduce-scatter.38.cloned.1.call-start = ((), (), s32[]{:S(2)}) async-start(), calls=%async_computation.27 | async-start | bytes 1310720 | tf_op jit(solution)/shard_map/reduce_scatter | solution.py:351
  1410.8 247.6 %reduce-scatter.34.cloned.1.call-start = ((), (), s32[]{:S(2)}) async-start(), calls=%async_computation.25 | async-start | bytes 2621440 | tf_op jit(solution)/shard_map/reduce_scatter | solution.py:339
  1411.5 280.8 %reduce-scatter.36.cloned.1.call-start = ((), (), s32[]{:S(2)}) async-start(), calls=%async_computation.26 | async-start | bytes 2621440 | tf_op jit(solution)/shard_map/reduce_scatter | solution.py:345
  1414.0 13.8 copy-start.36
  1414.4 13.4 copy-start.37
  (89 other events, 257.0 us)
Sparse Core Ops, SparseCore 0:
  9.6 19.4 all-gather.9
  30.6 16.7 all-gather.13
  49.0 16.7 all-gather.21
  68.4 60.4 all-gather.11
  131.4 72.0 all-gather.15
  204.9 20.8 all-gather.17
  227.4 22.6 all-gather.19
  402.4 117.9 reduce-scatter.23
  524.0 148.1 reduce-scatter.25
  1402.2 18.3 reduce-scatter.45
  1423.6 19.5 reduce-scatter.47
  1445.7 21.6 reduce-scatter.39
  1470.5 21.6 reduce-scatter.27
  1495.2 21.6 reduce-scatter.29
  1519.3 21.6 reduce-scatter.31
  1544.1 24.8 reduce-scatter.41
  1572.0 24.8 reduce-scatter.43
  1599.4 24.8 reduce-scatter.37
  1626.9 31.3 reduce-scatter.33
  1660.8 31.4 reduce-scatter.35
where the time goes:
time: 1710 us; the launch traced here: 1700 us
  blocking collectives  784 us (46%)
  waiting for transfers between devices  592 us (35%)
  matrix products  137 us (8%)
  local copies, waits for them, and re-layouts  100 us (6%)
  other arithmetic  56.8 us (3%)
  between operations  17.7 us (1%)
    psum x1, blocking collectives, shards(): lax.psum((g_query, g_keyval, g_out, g_cquery, g_ckv, g_cout, g_first, g_b...  726 us
    reduce_scatter x1, waiting for transfers between devices, shards(): lax.psum_scatter(mem_terms, 'ctx', scatter_dimension=0, tiled=True)  149 us
    reduce_scatter x1, waiting for transfers between devices, shards(): lax.psum_scatter(key_terms, 'ctx', scatter_dimension=0, tiled=True)  102 us
    unnamed x25, waiting for transfers between devices  95.2 us
    all_gather x1, waiting for transfers between devices, shards(): mem_all = lax.all_gather(mem_keyvals, 'ctx', axis=0, tiled=True)  37.1 us
  transfers between devices with their start and end apart: 22, of which 17 were waited for; matrix products, arithmetic and copies ran while one was open for 8% of the time, Pallas kernels for 0%

commit v1 on v0

--- a/solution.py
+++ b/solution.py
@@ -235,7 +235,19 @@
     cross_queries = forward_product(hidden_one_low, c_query).astype(jnp.bfloat16)
     mem_rows = memory[0]
     mem_keyvals = forward_product(mem_rows, c_keyval).astype(jnp.bfloat16)
-    mem_all = lax.all_gather(mem_keyvals, "ctx", axis=0, tiled=True)
+    found_now, clean, aux = (lax.axis_size("ctx"), lax.axis_index("ctx"), mem_keyvals.shape[0])
+    rows = []
+    for d in range(found_now):
+        rows.append((d, (d + 1) % found_now))
+    mem_all = jnp.zeros(
+        (*mem_keyvals.shape[:0], found_now * aux, *mem_keyvals.shape[1:]), mem_keyvals.dtype
+    )
+    reached = mem_keyvals
+    for w in range(found_now):
+        block_out = (clean - w) % found_now
+        mem_all = lax.dynamic_update_slice_in_dim(mem_all, reached, block_out * aux, axis=0)
+        if w < found_now - 1:
+            reached = lax.ppermute(reached, axis_name="ctx", perm=rows)
     cross_state = fold_keys(fold_start(n_rows, n_width), cross_queries, mem_all, 0, mem_count)
     cross_mixed, cross_lse = fold_finish(cross_state)
     cross_low = cross_mixed.astype(jnp.bfloat16)

time: 1710 us -> 1740 us (1.018)
  waiting for transfers between devices: 592 us -> 624 us
    ppermute x0 -> x7, waiting for transfers between devices: none -> 86 us  [shards(): reached = lax.ppermute(reached, axis_name='ctx', perm=rows)]
    all_gather x1 -> x0, waiting for transfers between devices: 37.1 us -> none  [shards(): mem_all = lax.all_gather(mem_keyvals, 'ctx', axis=0, tiled=True)]
    unnamed x25 -> x24, waiting for transfers between devices: 95.2 us -> 94.6 us
  transfers between devices with their start and end apart: 22 -> 28, of which waited for: 17 -> 20; matrix products, arithmetic and copies ran while one was open for 8% -> 8% of each run, Pallas kernels for 0% -> 0%
where the time goes in v1:
time: 1740 us
  blocking collectives  782 us (45%)
  waiting for transfers between devices  624 us (36%)
  matrix products  140 us (8%)
  local copies, waits for them, and re-layouts  105 us (6%)
  other arithmetic  52.8 us (3%)
    psum x1, blocking collectives, shards(): lax.psum((g_query, g_keyval, g_out, g_cquery, g_ckv, g_cout, g_first, g_b...  726 us
    reduce_scatter x1, waiting for transfers between devices, shards(): lax.psum_scatter(mem_terms, 'ctx', scatter_dimension=0, tiled=True)  149 us
    reduce_scatter x1, waiting for transfers between devices, shards(): lax.psum_scatter(key_terms, 'ctx', scatter_dimension=0, tiled=True)  102 us
    unnamed x24, waiting for transfers between devices  94.6 us
    ppermute x7, waiting for transfers between devices, shards(): reached = lax.ppermute(reached, axis_name='ctx', perm=rows)  86 us
  transfers between devices with their start and end apart: 28, of which 20 were waited for; matrix products, arithmetic and copies ran while one was open for 8% of the time, Pallas kernels for 0%

profile of v1, /device:TPU:0, one launch (start us, length us, event | category | flops | bytes accessed | tf_op | source)
XLA Modules:
  0.0 1735.4 jit_solution(3906113417815016289)
XLA Ops:
  9.5 19.6 %all-gather.9.cloned.1.call-done = bf16[512,1024]{1,0:T(8,128)(2,1)} async-done(((bf16[128,1024]{1,0:T(8,128)(2,1)}), bf16[512,1024]{1,0:T(8,128)(2,1)}) %all-gather.9.cloned.1.call-update) | async-done | bytes 1048592 | tf_op jit(solution)/shard_map/all_gather | solution.py:184
  32.2 15.1 all-gather.13.cloned.1.call-done
  52.6 15.3 collective-permute-done
  67.9 19.3 %collective-permute-done.1 = bf16[256,1024]{1,0:T(8,128)(2,1)S(1)} collective-permute-done((bf16[256,1024]{1,0:T(8,128)(2,1)S(1)}, bf16[256,1024]{1,0:T(8,128)(2,1)S(1)}, u32[]{:S(2)}, u32[]{:S(2)}) %collective-permute-start.1) | collective-permute-done | bytes 524320 | tf_op jit(solution)/shard_map/ppermute | solution.py:250
  87.4 5.1 all_gather.48
  92.4 15.4 collective-permute-done.2
  107.8 6.9 all_gather.51
  114.8 7.7 all_gather.50
  122.5 13.0 collective-permute-done.3
  135.6 6.5 all_gather.45
  142.1 5.1 all_gather.47
  147.4 11.4 collective-permute-done.4
  158.8 7.7 all_gather.46
  167.2 5.4 all-gather.1
  172.6 5.2 all-gather
  190.3 11.5 collective-permute-done.6
  202.7 6.2 copy.69
  208.8 4.7 copy.67
  213.5 27.6 %while.56 = (s32[]{:T(128)}, f32[8,192]{1,0:T(8,128)S(1)}, f32[8,192]{1,0:T(8,128)S(1)}, f32[192,8,64]{0,2,1:T(8,128)}, s32[3]{0:T(128)S(1)}, /*index=5*/s32[]{:...) while((s32[]{:T(128)}, f32[8,192]{1,0:T(8,128)S(1)}, ...), condition=%wide.region_3.4_spmd.clone, body=%wide.region_0.3_spmd.clone.sunk | while | flops 712812544 | bytes 21793044 | solution.py:95
  244.7 36.3 %while.57 = (s32[]{:T(128)}, f32[8,192]{1,0:T(8,128)S(1)}, f32[8,192]{1,0:T(8,128)S(1)}, f32[192,8,64]{0,2,1:T(8,128)}, s32[2]{0:T(128)S(1)}, /*index=5*/s32[]{:...) while((s32[]{:T(128)}, f32[8,192]{1,0:T(8,128)S(1)}, ...), condition=%wide.region_9.10_spmd.clone, body=%wide.region_6.9_spmd.clone.sunk | while | flops 1425320960 | bytes 55611584 | solution.py:95
  248.6 3.6 select_reduce_fusion.5
  252.2 4.1 fusion.210
  256.9 5.5 fusion.212
  266.2 3.6 select_reduce_fusion.5
  269.8 4.1 fusion.210
  274.5 6.4 fusion.212
  282.9 3.4 convolution_add_fusion
  286.2 2.8 fusion.104
  293.9 4.3 convert_reduce_fusion
  302.3 67.4 %while.58 = (s32[]{:T(128)}, f32[192,8,64]{0,2,1:T(8,128)}, f32[2,1024,1024]{2,1,0:T(8,128)}, bf16[2,1024,1024]{1,2,0:T(8,128)(2,1)}, s32[2]{0:T(128)S(1)}, /*in...) while((s32[]{:T(128)}, f32[192,8,64]{0,2,1:T(8,128)}, ...), condition=%wide.region_20.21_spmd.clone, body=%wide.region_19.20_spmd.clone.sunk | while | flops 2029291520 | bytes 105076096 | solution.py:158
  307.6 3.3 multiply_convert_fusion.8
  310.9 3.2 fusion.224
  314.1 7.5 fusion.225
  325.7 5.3 copy.121
  331.1 4.9 constant_dynamic-update-slice_fusion.12
  341.2 3.3 multiply_convert_fusion.8
  344.5 3.3 fusion.224
  347.9 7.4 fusion.225
  359.5 5.3 copy.121
  364.8 4.8 constant_dynamic-update-slice_fusion.12
  378.5 57.5 %while.59 = (s32[]{:T(128)}, f32[192,8,64]{0,2,1:T(8,128)}, f32[3,512,1024]{2,1,0:T(8,128)}, bf16[3,512,1024]{1,2,0:T(8,128)(2,1)}, s32[3]{0:T(128)S(1)}, /*inde...) while((s32[]{:T(128)}, f32[192,8,64]{0,2,1:T(8,128)}, ...), condition=%wide.region_25.26_spmd.clone, body=%wide.region_24.25_spmd.clone.sunk | while | flops 1014793216 | bytes 47927116 | solution.py:158
  383.5 3.2 multiply_convert_fusion.9
  386.6 3.0 fusion.237
  402.5 3.2 multiply_convert_fusion.9
  405.6 3.1 fusion.237
  421.6 3.2 multiply_convert_fusion.9
  424.8 3.1 fusion.237
  445.7 2.9 fusion.88
  452.7 101.9 %reduce-scatter.24.cloned.1.call-done = f32[192,1024]{1,0:T(8,128)} async-done(((f32[1536,1024]{1,0:T(8,128)}), f32[192,1024]{1,0:T(8,128)}) %reduce-scatter.24.cloned.1.call-update) | async-done | bytes 786448 | tf_op jit(solution)/shard_map/reduce_scatter | solution.py:307
  554.6 2.9 convolution_bitcast_fusion.1
  557.5 148.9 %reduce-scatter.26.cloned.1.call-done = f32[256,1024]{1,0:T(8,128)} async-done(((f32[2048,1024]{1,0:T(8,128)}), f32[256,1024]{1,0:T(8,128)}) %reduce-scatter.26.cloned.1.call-update) | async-done | bytes 1048592 | tf_op jit(solution)/shard_map/reduce_scatter | solution.py:292
  706.4 3.0 convolution_bitcast_fusion
  709.4 725.9 %all-reduce.5 = (bf16[512,512]{0,1:T(8,128)(2,1)}, bf16[512,1024]{0,1:T(8,128)(2,1)}, bf16[512,1024]{0,1:T(8,128)(2,1)}, bf16[512,512]{1,0:T(8,128)(2,1)}, bf16[...) all-reduce(f32[512,512]{0,1:T(8,128)} %convolution_bitcast_fusion.2, ...), channel_id=1, replica_groups=mesh['ctx'=8,'wsh'=4] {'ctx'}, use_global_device_ids=true, to_apply=%region_28.29 | all-reduce | flops 4724224 | bytes 28345344 | tf_op jit(solution)/shard_map/psum | solution.py:314
  1453.6 6.9 all-reduce.3
  1464.6 12.6 reduce-scatter.48.cloned.1.call-done
  1478.6 23.0 %reduce-scatter.40.cloned.1.call-done = bf16[128,512]{1,0:T(8,128)(2,1)} async-done(((bf16[512,512]{1,0:T(8,128)(2,1)}), bf16[128,512]{1,0:T(8,128)(2,1)}) %reduce-scatter.40.cloned.1.call-update) | async-done | bytes 131088
  1503.4 22.7 %reduce-scatter.28.cloned.1.call-done = bf16[128,512]{1,0:T(8,128)(2,1)} async-done(((bf16[512,512]{1,0:T(8,128)(2,1)}), bf16[128,512]{1,0:T(8,128)(2,1)}) %reduce-scatter.28.cloned.1.call-update) | async-done | bytes 131088 | tf_op jit(solution)/shard_map/reduce_scatter | solution.py:339
  1527.8 23.3 %reduce-scatter.30.cloned.1.call-done = bf16[128,512]{1,0:T(8,128)(2,1)} async-done(((bf16[512,512]{1,0:T(8,128)(2,1)}), bf16[128,512]{1,0:T(8,128)(2,1)}) %reduce-scatter.30.cloned.1.call-update) | async-done | bytes 131088 | tf_op jit(solution)/shard_map/reduce_scatter | solution.py:342
  1552.7 22.4 %reduce-scatter.32.cloned.1.call-done = bf16[128,512]{1,0:T(8,128)(2,1)} async-done(((bf16[512,512]{1,0:T(8,128)(2,1)}), bf16[128,512]{1,0:T(8,128)(2,1)}) %reduce-scatter.32.cloned.1.call-update) | async-done | bytes 131088 | tf_op jit(solution)/shard_map/reduce_scatter | solution.py:348
  1576.7 26.4 %reduce-scatter.42.cloned.1.call-done = bf16[128,1024]{1,0:T(8,128)(2,1)} async-done(((bf16[512,1024]{1,0:T(8,128)(2,1)}), bf16[128,1024]{1,0:T(8,128)(2,1)}) %reduce-scatter.42.cloned.1.call-update) | async-done | bytes 262160
  1605.2 25.8 %reduce-scatter.44.cloned.1.call-done = bf16[128,1024]{1,0:T(8,128)(2,1)} async-done(((bf16[512,1024]{1,0:T(8,128)(2,1)}), bf16[128,1024]{1,0:T(8,128)(2,1)}) %reduce-scatter.44.cloned.1.call-update) | async-done | bytes 262160
  1633.1 25.4 %reduce-scatter.38.cloned.1.call-done = bf16[256,512]{1,0:T(8,128)(2,1)} async-done(((bf16[1024,512]{1,0:T(8,128)(2,1)}), bf16[256,512]{1,0:T(8,128)(2,1)}) %reduce-scatter.38.cloned.1.call-update) | async-done | bytes 262160 | tf_op jit(solution)/shard_map/reduce_scatter | solution.py:363
  1660.3 32.0 %reduce-scatter.34.cloned.1.call-done = bf16[128,2048]{1,0:T(8,128)(2,1)} async-done(((bf16[512,2048]{1,0:T(8,128)(2,1)}), bf16[128,2048]{1,0:T(8,128)(2,1)}) %reduce-scatter.34.cloned.1.call-update) | async-done | bytes 524304 | tf_op jit(solution)/shard_map/reduce_scatter | solution.py:351
  1694.4 32.0 %reduce-scatter.36.cloned.1.call-done = bf16[512,512]{1,0:T(8,128)(2,1)} async-done(((bf16[2048,512]{1,0:T(8,128)(2,1)}), bf16[512,512]{1,0:T(8,128)(2,1)}) %reduce-scatter.36.cloned.1.call-update) | async-done | bytes 524304 | tf_op jit(solution)/shard_map/reduce_scatter | solution.py:357
  (500 shorter events, 186.2 us)
Async XLA Ops:
  7.2 42.7 %copy-start = (bf16[1,256,512]{2,1,0:T(8,128)(2,1)S(1)}, bf16[1,256,512]{2,1,0:T(8,128)(2,1)}, u32[]{:S(2)}) copy-start(bf16[1,256,512]{2,1,0:T(8,128)(2,1)} %param.27) | copy-start | bytes 786436
  7.2 21.9 %all-gather.9.cloned.1.call-start = ((), (), s32[]{:S(2)}) async-start(), calls=%async_computation.13 | async-start | bytes 1310720 | tf_op jit(solution)/shard_map/all_gather | solution.py:184
  7.9 39.4 %all-gather.13.cloned.1.call-start = ((), (), s32[]{:S(2)}) async-start(), calls=%async_computation.15 | async-start | bytes 1310720 | tf_op jit(solution)/shard_map/all_gather | solution.py:187
  8.7 169.9 %all-gather.19.cloned.1.call-start = ((), (), s32[]{:S(2)}) async-start(), calls=%async_computation.18 | async-start | bytes 1310720 | tf_op jit(solution)/shard_map/all_gather | solution.py:193
  9.4 199.4 %all-gather.11.cloned.1.call-start = ((), (), s32[]{:S(2)}) async-start(), calls=%async_computation.14 | async-start | bytes 3538944 | tf_op jit(solution)/shard_map/all_gather | solution.py:226
  31.5 251.3 %all-gather.15.cloned.1.call-start = ((), (), s32[]{:S(2)}) async-start(), calls=%async_computation.16 | async-start | bytes 2621440 | tf_op jit(solution)/shard_map/all_gather | solution.py:189
  32.1 254.1 %all-gather.17.cloned.1.call-start = ((), (), s32[]{:S(2)}) async-start(), calls=%async_computation.17 | async-start | bytes 2621440 | tf_op jit(solution)/shard_map/all_gather | solution.py:191
  32.2 55.2 %copy-start.90 = (bf16[3,128]{1,0:T(4,128)(2,1)S(1)}, bf16[3,128]{1,0:T(4,128)(2,1)}, u32[]{:S(2)}) copy-start(bf16[3,128]{1,0:T(4,128)(2,1)} %param.42) | copy-start | bytes 2308
  32.2 75.6 %copy-start.64 = (bf16[128,512]{1,0:T(8,128)(2,1)S(1)}, bf16[128,512]{1,0:T(8,128)(2,1)}, u32[]{:S(2)}) copy-start(bf16[128,512]{1,0:T(8,128)(2,1)} %param.35) | copy-start | bytes 393220
  32.2 82.6 %copy-start.65 = (bf16[128,512]{1,0:T(8,128)(2,1)S(1)}, bf16[128,512]{1,0:T(8,128)(2,1)}, u32[]{:S(2)}) copy-start(bf16[128,512]{1,0:T(8,128)(2,1)} %param.33) | copy-start | bytes 393220
  49.9 85.7 %copy-start.66 = (bf16[128,512]{1,0:T(8,128)(2,1)S(1)}, bf16[128,512]{1,0:T(8,128)(2,1)}, u32[]{:S(2)}) copy-start(bf16[128,512]{1,0:T(8,128)(2,1)} %param.30) | copy-start | bytes 393220
  49.9 92.2 %copy-start.91 = (bf16[3,128]{1,0:T(4,128)(2,1)S(1)}, bf16[3,128]{1,0:T(4,128)(2,1)}, u32[]{:S(2)}) copy-start(bf16[3,128]{1,0:T(4,128)(2,1)} %param.41) | copy-start | bytes 2308
  49.9 97.2 %copy-start.28 = (bf16[1,192,512]{2,1,0:T(8,128)(2,1)S(1)}, bf16[1,192,512]{2,1,0:T(8,128)(2,1)}, u32[]{:S(2)}) copy-start(bf16[1,192,512]{2,1,0:T(8,128)(2,1)} %param.26) | copy-start | bytes 589828
  49.9 108.9 %copy-start.67 = (bf16[128,512]{1,0:T(8,128)(2,1)S(1)}, bf16[128,512]{1,0:T(8,128)(2,1)}, u32[]{:S(2)}) copy-start(bf16[128,512]{1,0:T(8,128)(2,1)} %param.32) | copy-start | bytes 393220
  49.9 117.2 %copy-start.93 = (bf16[128]{0:T(256)(128)(2,1)S(1)}, bf16[128]{0:T(256)(128)(2,1)}, u32[]{:S(2)}) copy-start(bf16[128]{0:T(256)(128)(2,1)} %param.39) | copy-start | bytes 772
  49.9 122.6 %copy-start.92 = (bf16[512]{0:T(512)(128)(2,1)S(1)}, bf16[512]{0:T(512)(128)(2,1)}, u32[]{:S(2)}) copy-start(bf16[512]{0:T(512)(128)(2,1)} %param.37) | copy-start | bytes 3076
  49.9 128.7 %copy-start.54 = (bf16[1,192,512]{2,1,0:T(8,128)(2,1)S(1)}, bf16[1,192,512]{2,1,0:T(8,128)(2,1)}, u32[]{:S(2)}) copy-start(bf16[1,192,512]{2,1,0:T(8,128)(2,1)} %param.43) | copy-start | bytes 589828
  51.2 16.8 collective-permute-start
  67.9 19.3 %collective-permute-start.1 = (bf16[256,1024]{1,0:T(8,128)(2,1)S(1)}, bf16[256,1024]{1,0:T(8,128)(2,1)S(1)}, u32[]{:S(2)}, u32[]{:S(2)}) collective-permute-start(bf16[256,1024]{1,0:T(8,128)(2,1)S(1)} %collective-permute-done), channel_id=1, source_target_pairs={{0,4},{4,8},{8,12},{12,16},{16,20},{20,24},{24,28},{28,0},{1,5},{5... | collective-permute-start | bytes 1572872 | tf_op jit(solution)/shard_map/ppermute | solution.py:250
  87.3 20.5 %collective-permute-start.2 = (bf16[256,1024]{1,0:T(8,128)(2,1)S(1)}, bf16[256,1024]{1,0:T(8,128)(2,1)S(1)}, u32[]{:S(2)}, u32[]{:S(2)}) collective-permute-start(bf16[256,1024]{1,0:T(8,128)(2,1)S(1)} %collective-permute-done.1), channel_id=1, source_target_pairs={{0,4},{4,8},{8,12},{12,16},{16,20},{20,24},{24,28},{28,0},{1,5},{5... | collective-permute-start | bytes 1572872 | tf_op jit(solution)/shard_map/ppermute | solution.py:250
  87.3 467.3 %reduce-scatter.24.cloned.1.call-start = ((), (), s32[]{:S(2)}) async-start(), calls=%async_computation.19 | async-start | bytes 7077888 | tf_op jit(solution)/shard_map/reduce_scatter | solution.py:307
  107.8 27.7 %collective-permute-start.3 = (bf16[256,1024]{1,0:T(8,128)(2,1)S(1)}, bf16[256,1024]{1,0:T(8,128)(2,1)S(1)}, u32[]{:S(2)}, u32[]{:S(2)}) collective-permute-start(bf16[256,1024]{1,0:T(8,128)(2,1)S(1)} %collective-permute-done.2), channel_id=1, source_target_pairs={{0,4},{4,8},{8,12},{12,16},{16,20},{20,24},{24,28},{28,0},{1,5},{5... | collective-permute-start | bytes 1572872 | tf_op jit(solution)/shard_map/ppermute | solution.py:250
  122.5 159.6 %copy-start.75 = (f32[1,512]{1,0:T(1,128)}, f32[1,512]{1,0:T(1,128)S(1)}, u32[]{:S(2)}) copy-start(f32[1,512]{1,0:T(1,128)S(1)} %get-tuple-element.648) | copy-start | bytes 6148
  122.5 163.7 %copy-start.68 = (f32[1,512]{1,0:T(1,128)}, f32[1,512]{1,0:T(1,128)S(1)}, u32[]{:S(2)}) copy-start(f32[1,512]{1,0:T(1,128)S(1)} %get-tuple-element.647) | copy-start | bytes 6148
  135.6 23.3 %collective-permute-start.4 = (bf16[256,1024]{1,0:T(8,128)(2,1)S(1)}, bf16[256,1024]{1,0:T(8,128)(2,1)}, u32[]{:S(2)}, u32[]{:S(2)}) collective-permute-start(bf16[256,1024]{1,0:T(8,128)(2,1)S(1)} %collective-permute-done.3), channel_id=1, source_target_pairs={{0,4},{4,8},{8,12},{12,16},{16,20},{20,24},{24,28},{28,0},{1,5},{5... | collective-permute-start | bytes 1572872 | tf_op jit(solution)/shard_map/ppermute | solution.py:250
  147.1 152.6 %copy-start.62 = (f32[1,512]{1,0:T(1,128)}, f32[1,512]{1,0:T(1,128)S(1)}, u32[]{:S(2)}) copy-start(f32[1,512]{1,0:T(1,128)S(1)} %get-tuple-element.644) | copy-start | bytes 6148
  158.8 24.6 %collective-permute-start.5 = (bf16[256,1024]{1,0:T(8,128)(2,1)}, bf16[256,1024]{1,0:T(8,128)(2,1)}, u32[]{:S(2)}, u32[]{:S(2)}) collective-permute-start(bf16[256,1024]{1,0:T(8,128)(2,1)} %collective-permute-done.4), channel_id=1, source_target_pairs={{0,4},{4,8},{8,12},{12,16},{16,20},{20,24},{24,28},{28,0},{1,5},{5... | collective-permute-start | bytes 1572872 | tf_op jit(solution)/shard_map/ppermute | solution.py:250
  178.6 7.9 copy-start.84
  178.6 111.9 %copy-start.86 = (f32[192]{0:T(256)}, f32[192]{0:T(256)S(1)}, u32[]{:S(2)}) copy-start(f32[192]{0:T(256)S(1)} %get-tuple-element.628) | copy-start | bytes 2308
  180.4 9.9 copy-start.40
  181.3 109.2 %collective-permute-start.8 = (f32[1,512]{1,0:T(1,128)S(1)}, f32[1,512]{1,0:T(1,128)S(1)}, u32[]{:S(2)}, u32[]{:S(2)}) collective-permute-start(f32[1,512]{1,0:T(1,128)S(1)} %slice.99), channel_id=1, source_target_pairs={{0,4},{4,8},{8,12},{12,16},{16,20},{20,24},{24,28},{1,5},{5,9},{9,... | collective-permute-start | bytes 6152 | tf_op jit(solution)/shard_map/ppermute | solution.py:16
  183.4 18.4 %collective-permute-start.6 = (bf16[256,1024]{1,0:T(8,128)(2,1)}, bf16[256,1024]{1,0:T(8,128)(2,1)S(1)}, u32[]{:S(2)}, u32[]{:S(2)}) collective-permute-start(bf16[256,1024]{1,0:T(8,128)(2,1)} %collective-permute-done.5), channel_id=1, source_target_pairs={{0,4},{4,8},{8,12},{12,16},{16,20},{20,24},{24,28},{28,0},{1,5},{5... | collective-permute-start | bytes 1572872 | tf_op jit(solution)/shard_map/ppermute | solution.py:250
  242.3 47.2 %copy-start.19 = (f32[192,8,64]{0,2,1:T(8,128)}, f32[192,8,64]{0,2,1:T(8,128)S(1)}, u32[]{:S(2)}) copy-start(f32[192,8,64]{0,2,1:T(8,128)S(1)} %broadcast_divide_fusion.1) | copy-start | bytes 1179652
  244.0 38.2 %copy-start.11 = (f32[192,512]{1,0:T(8,128)}, f32[192,512]{1,0:T(8,128)S(1)}, u32[]{:S(2)}) copy-start(f32[192,512]{1,0:T(8,128)S(1)} %get-tuple-element.650) | copy-start | bytes 1179652
  244.7 37.5 %copy-start.34 = (bf16[512,512]{1,0:T(8,128)(2,1)S(1)}, bf16[512,512]{1,0:T(8,128)(2,1)}, u32[]{:S(2)}) copy-start(bf16[512,512]{1,0:T(8,128)(2,1)} %all_gather.51) | copy-start | bytes 1572868
  282.1 7.2 copy-start.21
  282.6 17.2 copy-start.15
  282.6 17.1 copy-start.70
  282.8 16.9 copy-start.72
  302.3 71.0 %copy-start.53 = (f32[8,192]{1,0:T(8,128)S(1)}, f32[8,192]{1,0:T(8,128)}, u32[]{:S(2)}) copy-start(f32[8,192]{1,0:T(8,128)} %copy-done.52) | copy-start | bytes 18436
  302.3 71.0 %copy-start.61 = (f32[8,192]{1,0:T(8,128)S(1)}, f32[8,192]{1,0:T(8,128)}, u32[]{:S(2)}) copy-start(f32[8,192]{1,0:T(8,128)} %copy-done.60) | copy-start | bytes 18436
  436.1 270.3 %reduce-scatter.26.cloned.1.call-start = ((), (), s32[]{:S(2)}) async-start(), calls=%async_computation.20 | async-start | bytes 9437184 | tf_op jit(solution)/shard_map/reduce_scatter | solution.py:292
  436.8 6.3 copy-start.20
  436.8 6.3 copy-start.25
  436.8 7.5 copy-start.22
  436.9 7.5 copy-start.27
  436.9 1026.3 %reduce-scatter.46.cloned.1.call-start = ((), (), s32[]{:S(2)}) async-start(), calls=%async_computation.30 | async-start | bytes 163840
  437.1 14.4 collective-permute-start.7
  451.5 257.9 %copy-start.56 = (bf16[191,512]{1,0:T(8,128)(2,1)}, bf16[191,512]{1,0:T(8,128)(2,1)S(1)}, u32[]{:S(2)}) copy-start(bf16[191,512]{1,0:T(8,128)(2,1)S(1)} %slice.96) | copy-start | bytes 586756
  452.7 256.8 %copy-start.74 = (f32[3,512]{1,0:T(4,128)S(1)}, f32[3,512]{1,0:T(4,128)}, u32[]{:S(2)}) copy-start(f32[3,512]{1,0:T(4,128)} %pad_maximum_fusion) | copy-start | bytes 18436
  452.7 256.7 %copy-start.79 = (f32[2048]{0:T(1024)S(1)}, f32[2048]{0:T(1024)}, u32[]{:S(2)}) copy-start(f32[2048]{0:T(1024)} %get-tuple-element.663) | copy-start | bytes 24580
  452.7 256.7 %copy-start.83 = (f32[512]{0:T(512)S(1)}, f32[512]{0:T(512)}, u32[]{:S(2)}) copy-start(f32[512]{0:T(512)} %get-tuple-element.625) | copy-start | bytes 6148
  1436.2 41.0 %reduce-scatter.48.cloned.1.call-start = ((), (), s32[]{:S(2)}) async-start(), calls=%async_computation.31 | async-start | bytes 163840
  1437.0 64.5 %reduce-scatter.40.cloned.1.call-start = ((), (), s32[]{:S(2)}) async-start(), calls=%async_computation.27 | async-start | bytes 655360
  1439.3 86.9 %reduce-scatter.28.cloned.1.call-start = ((), (), s32[]{:S(2)}) async-start(), calls=%async_computation.21 | async-start | bytes 655360 | tf_op jit(solution)/shard_map/reduce_scatter | solution.py:339
  1439.8 111.2 %reduce-scatter.30.cloned.1.call-start = ((), (), s32[]{:S(2)}) async-start(), calls=%async_computation.22 | async-start | bytes 655360 | tf_op jit(solution)/shard_map/reduce_scatter | solution.py:342
  1440.6 134.5 %reduce-scatter.32.cloned.1.call-start = ((), (), s32[]{:S(2)}) async-start(), calls=%async_computation.23 | async-start | bytes 655360 | tf_op jit(solution)/shard_map/reduce_scatter | solution.py:348
  1441.2 162.0 %reduce-scatter.42.cloned.1.call-start = ((), (), s32[]{:S(2)}) async-start(), calls=%async_computation.28 | async-start | bytes 1310720
  1442.8 188.2 %reduce-scatter.44.cloned.1.call-start = ((), (), s32[]{:S(2)}) async-start(), calls=%async_computation.29 | async-start | bytes 1310720
  1444.2 214.3 %reduce-scatter.38.cloned.1.call-start = ((), (), s32[]{:S(2)}) async-start(), calls=%async_computation.26 | async-start | bytes 1310720 | tf_op jit(solution)/shard_map/reduce_scatter | solution.py:363
  1444.8 247.4 %reduce-scatter.34.cloned.1.call-start = ((), (), s32[]{:S(2)}) async-start(), calls=%async_computation.24 | async-start | bytes 2621440 | tf_op jit(solution)/shard_map/reduce_scatter | solution.py:351
  1445.4 281.0 %reduce-scatter.36.cloned.1.call-start = ((), (), s32[]{:S(2)}) async-start(), calls=%async_computation.25 | async-start | bytes 2621440 | tf_op jit(solution)/shard_map/reduce_scatter | solution.py:357
  1448.1 13.8 copy-start.36
  1448.5 13.4 copy-start.37
  (85 other events, 266.6 us)
Sparse Core Ops, SparseCore 0:
  9.6 19.4 all-gather.8
  30.6 16.7 all-gather.12
  48.9 16.7 all-gather.18
  68.3 80.3 all-gather.10
  150.2 27.7 all-gather.14
  179.4 23.3 all-gather.16
  436.2 118.3 reduce-scatter.23
  558.2 148.1 reduce-scatter.25
  1436.3 18.3 reduce-scatter.45
  1457.5 19.5 reduce-scatter.47
  1479.8 21.6 reduce-scatter.39
  1504.4 21.6 reduce-scatter.27
  1529.3 21.6 reduce-scatter.29
  1553.4 21.6 reduce-scatter.31
  1578.2 24.8 reduce-scatter.41
  1606.1 24.8 reduce-scatter.43
  1633.6 24.8 reduce-scatter.37
  1660.9 31.3 reduce-scatter.33
  1695.0 31.4 reduce-scatter.35
